TPU v7x, 32 devices: a whole 2x2x4 slice. The times are simulated.
32 devices in a mesh: row: 4 (over z), col: 8 (over y, x, core).
Axes of the slice: x: 2, y: 2, z: 4, core: 2. Of those that a mesh axis runs over, the one named last changes fastest.
Arguments:
- factor_panel: bfloat16 [1024, 8192], P('row', 'col'), may hold values from -0.1875 to 0.1875
- ancestor_inv: float32 [1024, 1024], P('row', 'col'), may hold values from -6 to 6
- diag_inverse: float32 [4096, 8192], P('row', 'col'), may hold values from -6 to 6
- structure: int32 [2, 4], replicated, may hold values 0 or 1
Outputs:
- inverse_panel: float32 [1024, 8192], P('row', 'col')
- diag_sigma: float32 [4096, 8192], P('row', 'col')
All inputs are finite; a program needn't handle non-finite values.
Results may differ from a plain program's by a relative error of at most 0.0003.
Values may be sent and summed in bfloat16 or wider, within the bound.
A program may use at most 128 MiB of HBM per device.

v0:
```python
import jax
import jax.numpy as jnp
from jax import lax
from jax.sharding import PartitionSpec as P

B = 256
NS = 2


def local(factor_panel, ancestor_inv, diag_inverse, structure):
    rows_dev, width_dev = factor_panel.shape
    per_block = width_dev // NS
    row_index = lax.axis_index("row")
    keep_tiles = jnp.repeat(structure, B, axis=1)
    keep_own = lax.dynamic_slice_in_dim(keep_tiles, row_index * rows_dev, rows_dev, 1)
    keep_cols = jnp.repeat(keep_own.T, per_block, axis=1)
    lhat_local = jnp.where(keep_cols == 1, factor_panel, jnp.zeros_like(factor_panel))
    column = lax.all_gather(lhat_local, "row", axis=0, tiled=True)
    sigma_rows = lax.all_gather(ancestor_inv, "col", axis=1, tiled=True)
    column_wide = column.astype(jnp.float32)
    running = jnp.dot(sigma_rows, column_wide, precision=lax.Precision.HIGHEST)
    inverse_panel = jnp.where(keep_cols == 1, -running, jnp.zeros_like(running))
    rows_all = lax.all_gather(lhat_local, "col", axis=1, tiled=True)
    block_count = rows_all.shape[1] // width_dev
    rows_cube = rows_all.reshape(rows_dev, block_count, NS, per_block)
    lhat_members = [
        rows_cube[:, :, member, :].reshape(rows_dev, block_count * per_block).astype(jnp.float32)
        for member in range(NS)
    ]
    pieces = []
    for member in range(NS):
        window = lhat_members[member]
        target = inverse_panel[:, member * per_block : (member + 1) * per_block]
        pieces.append(
            lax.dot_general(
                window,
                target,
                (((0,), (0,)), ((), ())),
                precision=lax.Precision.HIGHEST,
                preferred_element_type=jnp.float32,
            )
        )
    update = lax.psum_scatter(
        jnp.concatenate(pieces, axis=1), "row", scatter_dimension=0, tiled=True
    )
    diag_sigma = diag_inverse - update
    return (inverse_panel, diag_sigma)


def solution(mesh):
    placed = (P("row", "col"), P("row", "col"), P("row", "col"), P())
    return jax.shard_map(
        local,
        mesh=mesh,
        in_specs=placed,
        out_specs=(P("row", "col"), P("row", "col")),
        check_vma=False,
    )
```

profile of v0, /device:TPU:0, one launch (start us, length us, event | category | flops | bytes accessed | tf_op | source)
XLA Modules:
  0.0 437.1 jit_solution(3430236630493984573)
XLA Ops:
  7.2 0.0 copy-start
  7.2 0.0 all-gather.6.cloned.1.call-start
  7.2 0.7 all-gather.6.cloned.1.call-update
  7.9 0.0 all-gather.4.cloned.1.call-start
  8.0 0.0 copy-done
  8.0 0.1 broadcast_bitcast_fusion
  8.1 1.2 copy.6
  9.3 0.8 bitcast_select_fusion.1
  10.2 0.0 all-gather.4.cloned.1.call-update
  10.2 0.0 all-gather.8.cloned.1.call-start
  10.2 0.7 all-gather.8.cloned.1.call-update
  10.9 0.0 reduce-scatter.2.cloned.1.call-start
  11.0 25.2 %all-gather.6.cloned.1.call-done = f32[256,1024]{1,0:T(8,128)} async-done(((f32[256,128]{1,0:T(8,128)}), f32[256,1024]{1,0:T(8,128)}) %all-gather.6.cloned.1.call-update) | async-done | bytes 1048592 | tf_op jit(solution)/shard_map/all_gather | solution.py:19
  36.2 48.4 %all-gather.4.cloned.1.call-done = bf16[1024,1024]{0,1:T(8,128)(2,1)} async-done(((bf16[256,1024]{0,1:T(8,128)(2,1)}), bf16[1024,1024]{0,1:T(8,128)(2,1)}) %all-gather.4.cloned.1.call-update) | async-done | bytes 2097168 | tf_op jit(solution)/shard_map/all_gather | solution.py:18
  84.6 3.7 bitcast_select_fusion
  88.3 33.7 %all-gather.8.cloned.1.call-done = bf16[256,8192]{0,1:T(8,128)(2,1)} async-done(((bf16[256,1024]{0,1:T(8,128)(2,1)}), bf16[256,8192]{0,1:T(8,128)(2,1)}) %all-gather.8.cloned.1.call-update) | async-done | bytes 4194320 | tf_op jit(solution)/shard_map/all_gather | solution.py:23
  122.1 2.6 fusion.5
  124.6 3.5 fusion.1
  128.1 3.5 fusion.3
  131.6 6.4 %pad_maximum_fusion = f32[4096,1024]{0,1:T(8,128)} fusion(f32[4096,512]{0,1:T(8,128)S(1)} %fusion.1, f32[4096,512]{0,1:T(8,128)S(1)} %fusion.3), kind=kLoop, calls=%fused_computation | loop fusion | flops 4194304 | bytes 33554432 | tf_op jit(solution)/shard_map/concatenate | solution.py:44
  138.0 0.0 reduce-scatter.2.cloned.1.call-update
  138.0 5.3 %copy.7 = f32[1024,1024]{0,1:T(8,128)} copy(f32[1024,1024]{1,0:T(8,128)} %param.6) | data formatting | bytes 8388608 | tf_op args[2]
  143.3 1.3 copy.8
  144.6 273.8 %reduce-scatter.2.cloned.1.call-done = f32[1024,1024]{0,1:T(8,128)} async-done(((f32[4096,1024]{0,1:T(8,128)}), f32[1024,1024]{0,1:T(8,128)}) %reduce-scatter.2.cloned.1.call-update) | async-done | bytes 4194320 | tf_op jit(solution)/shard_map/reduce_scatter | solution.py:43
  418.4 0.0 copy-start.1
  418.4 6.8 %sub.3 = f32[1024,1024]{0,1:T(8,128)} subtract(f32[1024,1024]{0,1:T(8,128)} %copy.7, f32[1024,1024]{0,1:T(8,128)} %reduce-scatter.2.cloned.1.call-done) | non-fusion elementwise | flops 1048576 | bytes 12582912 | tf_op jit(solution)/shard_map/sub | solution.py:46
  425.2 5.3 %copy.9 = f32[1024,1024]{1,0:T(8,128)} copy(f32[1024,1024]{0,1:T(8,128)} %sub.3) | data formatting | bytes 8388608
  430.6 0.0 copy-done.1
  (2 shorter events, 0.0 us)
Async XLA Ops:
  7.2 0.8 copy-start
  7.2 29.0 %all-gather.6.cloned.1.call-start = ((), (), s32[]{:S(2)}) async-start(), calls=%async_computation.2 | async-start | bytes 1179648 | tf_op jit(solution)/shard_map/all_gather | solution.py:19
  7.9 76.7 %all-gather.4.cloned.1.call-start = ((), (), s32[]{:S(2)}) async-start(), calls=%async_computation.1 | async-start | bytes 2621440 | tf_op jit(solution)/shard_map/all_gather | solution.py:18
  10.2 111.9 %all-gather.8.cloned.1.call-start = ((), (), s32[]{:S(2)}) async-start(), calls=%async_computation.3 | async-start | bytes 4718592 | tf_op jit(solution)/shard_map/all_gather | solution.py:23
  10.9 407.5 %reduce-scatter.2.cloned.1.call-start = ((), (), s32[]{:S(2)}) async-start(), calls=%async_computation.4 | async-start | bytes 20971520 | tf_op jit(solution)/shard_map/reduce_scatter | solution.py:43
  418.4 12.1 %copy-start.1 = (s32[2,4]{1,0:T(2,128)S(1)}, s32[2,4]{1,0:T(2,128)}, u32[]{:S(2)}) copy-start(s32[2,4]{1,0:T(2,128)} %param.7) | copy-start | bytes 100
Sparse Core Ops, SparseCore 0:
  9.9 26.2 all-gather.5
  38.3 46.2 all-gather.3
  87.1 34.9 all-gather.7
  138.1 280.2 reduce-scatter.1
where the time goes:
time: 437 us
  waiting for transfers between devices  383 us (88%)
  local copies, waits for them, and re-layouts  15.9 us (4%)
  other arithmetic  14 us (3%)
  between operations  13.8 us (3%)
  matrix products  10.6 us (2%)
    reduce_scatter x1, waiting for transfers between devices, local(): lax.psum_scatter(jnp.concatenate(pieces, axis=1), 'row', scatter_dimensio...  274 us
    all_gather x1, waiting for transfers between devices, local(): column = lax.all_gather(lhat_local, 'row', axis=0, tiled=True)  48.4 us
    all_gather x1, waiting for transfers between devices, local(): rows_all = lax.all_gather(lhat_local, 'col', axis=1, tiled=True)  33.7 us
    all_gather x1, waiting for transfers between devices, local(): sigma_rows = lax.all_gather(ancestor_inv, 'col', axis=1, tiled=True)  25.2 us
    unnamed x10, local copies, waits for them, and re-layouts  13.3 us
  transfers between devices with their start and end apart: 4, of which 4 were waited for; matrix products, arithmetic and copies ran while one was open for 3% of the time, Pallas kernels for 0%

commit v1 on v0

--- a/solution.py
+++ b/solution.py
@@ -2,9 +2,26 @@
 import jax.numpy as jnp
 from jax import lax
 from jax.sharding import PartitionSpec as P
+from jax.lax import axis_index, axis_size, ppermute
 
 B = 256
 NS = 2
+
+
+def report_notes_by_axis(panel, shard_axis):
+    n_slots = axis_size(shard_axis)
+    trail = tuple(((q, (q + 1) % n_slots) for q in range(n_slots)))
+
+    def targets_step_on(last):
+        if len(last) == n_slots:
+            return last
+        return targets_step_on([ppermute(last[0], shard_axis, trail), *last])
+
+    return jnp.roll(
+        jnp.concatenate(targets_step_on([panel]), axis=1),
+        shift=(axis_index(shard_axis) + 1) * panel.shape[1],
+        axis=1,
+    )
 
 
 def local(factor_panel, ancestor_inv, diag_inverse, structure):
@@ -20,7 +37,7 @@
     column_wide = column.astype(jnp.float32)
     running = jnp.dot(sigma_rows, column_wide, precision=lax.Precision.HIGHEST)
     inverse_panel = jnp.where(keep_cols == 1, -running, jnp.zeros_like(running))
-    rows_all = lax.all_gather(lhat_local, "col", axis=1, tiled=True)
+    rows_all = report_notes_by_axis(lhat_local, "col")
     block_count = rows_all.shape[1] // width_dev
     rows_cube = rows_all.reshape(rows_dev, block_count, NS, per_block)
     lhat_members = [

time: 437 us -> 409 us (0.936)
  waiting for transfers between devices: 383 us -> 349 us
  local copies, waits for them, and re-layouts: 15.9 us -> 20.8 us
    ppermute x0 -> x7, waiting for transfers between devices: none -> 60 us  [targets_step_on(): return targets_step_on([ppermute(last[0], shard_axis, trail), *last])]
    all_gather x1 -> x0, waiting for transfers between devices: 33.7 us -> none  [local(): rows_all = lax.all_gather(lhat_local, 'col', axis=1, tiled=True)]
    all_gather x1, waiting for transfers between devices: 48.4 us -> 16.2 us  [local(): column = lax.all_gather(lhat_local, 'row', axis=0, tiled=True)]
    all_gather x1, waiting for transfers between devices: 25.2 us -> 0.01 us  [local(): sigma_rows = lax.all_gather(ancestor_inv, 'col', axis=1, tiled=True)]
    unnamed x10 -> x37, local copies, waits for them, and re-layouts: 13.3 us -> 20.2 us
  transfers between devices with their start and end apart: 4 -> 10, of which waited for: 4 -> 8; matrix products, arithmetic and copies ran while one was open for 3% -> 3% of each run, Pallas kernels for 0% -> 0%
where the time goes in v1:
time: 409 us
  waiting for transfers between devices  349 us (85%)
  local copies, waits for them, and re-layouts  20.8 us (5%)
  between operations  14 us (3%)
  other arithmetic  13.4 us (3%)
  matrix products  10.7 us (3%)
    reduce_scatter x1, waiting for transfers between devices, local(): lax.psum_scatter(jnp.concatenate(pieces, axis=1), 'row', scatter_dimensio...  272 us
    ppermute x7, waiting for transfers between devices, targets_step_on(): return targets_step_on([ppermute(last[0], shard_axis, trail), *last])  60 us
    unnamed x37, local copies, waits for them, and re-layouts  20.2 us
    all_gather x1, waiting for transfers between devices, local(): column = lax.all_gather(lhat_local, 'row', axis=0, tiled=True)  16.2 us
  transfers between devices with their start and end apart: 10, of which 8 were waited for; matrix products, arithmetic and copies ran while one was open for 3% of the time, Pallas kernels for 0%

profile of v1, /device:TPU:0, one launch (start us, length us, event | category | flops | bytes accessed | tf_op | source)
XLA Modules:
  0.0 408.5 jit_solution(14803953793508106924)
XLA Ops:
  7.2 0.0 copy-start
  7.2 0.0 all-gather.5.cloned.1.call-start
  7.2 0.7 all-gather.5.cloned.1.call-update
  7.9 0.0 all-gather.3.cloned.1.call-start
  8.0 0.0 copy-done
  8.0 0.1 broadcast_bitcast_fusion
  8.1 1.2 copy.6
  9.4 0.0 copy-start.2
  9.4 0.5 collective-permute-start
  9.9 9.7 %collective-permute-done = bf16[256,1024]{0,1:T(8,128)(2,1)S(1)} collective-permute-done((bf16[256,1024]{0,1:T(8,128)(2,1)S(1)}, bf16[256,1024]{0,1:T(8,128)(2,1)S(1)}, u32[]{:S(2)}, u32[]{:S(2)}) %collective-permute-start) | collective-permute-done | bytes 524320 | tf_op jit(solution)/shard_map/ppermute | solution.py:18
  19.6 0.0 collective-permute-start.1
  19.6 0.0 copy-done.2
  19.6 0.0 all-gather.3.cloned.1.call-update
  19.7 0.0 copy-start.3
  19.7 0.0 reduce-scatter.2.cloned.1.call-start
  19.7 10.8 %collective-permute-done.1 = bf16[256,1024]{0,1:T(8,128)(2,1)S(1)} collective-permute-done((bf16[256,1024]{0,1:T(8,128)(2,1)S(1)}, bf16[256,1024]{0,1:T(8,128)(2,1)S(1)}, u32[]{:S(2)}, u32[]{:S(2)}) %collective-permute-start.1) | collective-permute-done | bytes 524320 | tf_op jit(solution)/shard_map/ppermute | solution.py:18
  30.6 0.0 collective-permute-start.2
  30.6 10.9 %collective-permute-done.2 = bf16[256,1024]{0,1:T(8,128)(2,1)S(1)} collective-permute-done((bf16[256,1024]{0,1:T(8,128)(2,1)S(1)}, bf16[256,1024]{0,1:T(8,128)(2,1)S(1)}, u32[]{:S(2)}, u32[]{:S(2)}) %collective-permute-start.2) | collective-permute-done | bytes 524320 | tf_op jit(solution)/shard_map/ppermute | solution.py:18
  41.4 0.0 collective-permute-start.3
  41.4 9.5 %collective-permute-done.3 = bf16[256,1024]{0,1:T(8,128)(2,1)S(1)} collective-permute-done((bf16[256,1024]{0,1:T(8,128)(2,1)S(1)}, bf16[256,1024]{0,1:T(8,128)(2,1)S(1)}, u32[]{:S(2)}, u32[]{:S(2)}) %collective-permute-start.3) | collective-permute-done | bytes 524320 | tf_op jit(solution)/shard_map/ppermute | solution.py:18
  50.9 0.0 collective-permute-start.4
  50.9 9.5 %collective-permute-done.4 = bf16[256,1024]{0,1:T(8,128)(2,1)S(1)} collective-permute-done((bf16[256,1024]{0,1:T(8,128)(2,1)S(1)}, bf16[256,1024]{0,1:T(8,128)(2,1)S(1)}, u32[]{:S(2)}, u32[]{:S(2)}) %collective-permute-start.4) | collective-permute-done | bytes 524320 | tf_op jit(solution)/shard_map/ppermute | solution.py:18
  60.4 0.0 collective-permute-start.5
  60.4 9.6 %collective-permute-done.5 = bf16[256,1024]{0,1:T(8,128)(2,1)} collective-permute-done((bf16[256,1024]{0,1:T(8,128)(2,1)S(1)}, bf16[256,1024]{0,1:T(8,128)(2,1)}, u32[]{:S(2)}, u32[]{:S(2)}) %collective-permute-start.5) | collective-permute-done | bytes 524320 | tf_op jit(solution)/shard_map/ppermute | solution.py:18
  70.0 0.0 collective-permute-start.6
  70.0 0.0 copy-done.4
  70.0 0.0 copy-done.6
  70.1 16.2 %all-gather.3.cloned.1.call-done = bf16[1024,1024]{0,1:T(8,128)(2,1)} async-done(((bf16[256,1024]{0,1:T(8,128)(2,1)}), bf16[1024,1024]{0,1:T(8,128)(2,1)}) %all-gather.3.cloned.1.call-update) | async-done | bytes 2097168 | tf_op jit(solution)/shard_map/all_gather | solution.py:35
  86.3 3.8 bitcast_select_fusion
  90.1 0.0 collective-permute-done.6
  90.1 1.1 constant_dynamic-update-slice_fusion.15
  91.2 1.1 constant_dynamic-update-slice_fusion.14
  92.2 1.1 constant_dynamic-update-slice_fusion.13
  93.3 1.1 constant_dynamic-update-slice_fusion.12
  94.6 1.1 constant_dynamic-update-slice_fusion.7
  95.7 1.1 constant_dynamic-update-slice_fusion.6
  96.8 0.0 copy-done.5
  97.0 0.3 constant_dynamic-slice_fusion
  97.3 0.4 fusion.5
  97.7 3.5 fusion.3
  101.2 3.5 fusion.1
  104.6 6.5 %pad_maximum_fusion = f32[4096,1024]{0,1:T(8,128)} fusion(f32[4096,512]{0,1:T(8,128)S(1)} %fusion.1, f32[4096,512]{0,1:T(8,128)S(1)} %fusion.3), kind=kLoop, calls=%fused_computation | loop fusion | flops 4194304 | bytes 33554432 | tf_op jit(solution)/shard_map/concatenate | solution.py:61
  111.2 0.0 reduce-scatter.2.cloned.1.call-update
  111.2 5.3 %copy.7 = f32[1024,1024]{0,1:T(8,128)} copy(f32[1024,1024]{1,0:T(8,128)} %param.6) | data formatting | bytes 8388608 | tf_op args[2]
  116.6 1.3 copy.8
  117.9 272.0 %reduce-scatter.2.cloned.1.call-done = f32[1024,1024]{0,1:T(8,128)} async-done(((f32[4096,1024]{0,1:T(8,128)}), f32[1024,1024]{0,1:T(8,128)}) %reduce-scatter.2.cloned.1.call-update) | async-done | bytes 4194320 | tf_op jit(solution)/shard_map/reduce_scatter | solution.py:60
  389.9 6.8 %sub.8 = f32[1024,1024]{0,1:T(8,128)} subtract(f32[1024,1024]{0,1:T(8,128)} %copy.7, f32[1024,1024]{0,1:T(8,128)} %reduce-scatter.2.cloned.1.call-done) | non-fusion elementwise | flops 1048576 | bytes 12582912 | tf_op jit(solution)/shard_map/sub | solution.py:63
  396.7 5.3 %copy.9 = f32[1024,1024]{1,0:T(8,128)} copy(f32[1024,1024]{0,1:T(8,128)} %sub.8) | data formatting | bytes 8388608
  (22 shorter events, 0.4 us)
Async XLA Ops:
  7.2 0.8 copy-start
  7.2 62.9 %all-gather.5.cloned.1.call-start = ((), (), s32[]{:S(2)}) async-start(), calls=%async_computation.2 | async-start | bytes 1179648 | tf_op jit(solution)/shard_map/all_gather | solution.py:36
  7.9 78.3 %all-gather.3.cloned.1.call-start = ((), (), s32[]{:S(2)}) async-start(), calls=%async_computation.1 | async-start | bytes 2621440 | tf_op jit(solution)/shard_map/all_gather | solution.py:35
  9.4 10.3 %copy-start.2 = (bf16[256,1024]{0,1:T(8,128)(2,1)}, bf16[256,1024]{0,1:T(8,128)(2,1)S(1)}, u32[]{:S(2)}) copy-start(bf16[256,1024]{0,1:T(8,128)(2,1)S(1)} %bitcast_select_fusion.1) | copy-start | bytes 1572868
  9.4 10.3 %collective-permute-start = (bf16[256,1024]{0,1:T(8,128)(2,1)S(1)}, bf16[256,1024]{0,1:T(8,128)(2,1)S(1)}, u32[]{:S(2)}, u32[]{:S(2)}) collective-permute-start(bf16[256,1024]{0,1:T(8,128)(2,1)S(1)} %bitcast_select_fusion.1), channel_id=1, source_target_pairs={{0,1},{1,2},{2,3},{3,4},{4,5},{5,6},{6,7},{7,0},{8,9},{9,10},{10,1... | collective-permute-start | bytes 1572872 | tf_op jit(solution)/shard_map/ppermute | solution.py:18
  19.6 10.9 %collective-permute-start.1 = (bf16[256,1024]{0,1:T(8,128)(2,1)S(1)}, bf16[256,1024]{0,1:T(8,128)(2,1)S(1)}, u32[]{:S(2)}, u32[]{:S(2)}) collective-permute-start(bf16[256,1024]{0,1:T(8,128)(2,1)S(1)} %collective-permute-done), channel_id=1, source_target_pairs={{0,1},{1,2},{2,3},{3,4},{4,5},{5,6},{6,7},{7,0},{8,9},{9,10},{10,1... | collective-permute-start | bytes 1572872 | tf_op jit(solution)/shard_map/ppermute | solution.py:18
  19.7 74.9 %copy-start.3 = (bf16[256,1024]{0,1:T(8,128)(2,1)S(1)}, bf16[256,1024]{0,1:T(8,128)(2,1)}, u32[]{:S(2)}) copy-start(bf16[256,1024]{0,1:T(8,128)(2,1)} %copy-done.2) | copy-start | bytes 1572868
  19.7 370.2 %reduce-scatter.2.cloned.1.call-start = ((), (), s32[]{:S(2)}) async-start(), calls=%async_computation.3 | async-start | bytes 20971520 | tf_op jit(solution)/shard_map/reduce_scatter | solution.py:60
  30.6 10.9 %collective-permute-start.2 = (bf16[256,1024]{0,1:T(8,128)(2,1)S(1)}, bf16[256,1024]{0,1:T(8,128)(2,1)S(1)}, u32[]{:S(2)}, u32[]{:S(2)}) collective-permute-start(bf16[256,1024]{0,1:T(8,128)(2,1)S(1)} %collective-permute-done.1), channel_id=1, source_target_pairs={{0,1},{1,2},{2,3},{3,4},{4,5},{5,6},{6,7},{7,0},{8,9},{9,10},{10,1... | collective-permute-start | bytes 1572872 | tf_op jit(solution)/shard_map/ppermute | solution.py:18
  41.4 9.5 %collective-permute-start.3 = (bf16[256,1024]{0,1:T(8,128)(2,1)S(1)}, bf16[256,1024]{0,1:T(8,128)(2,1)S(1)}, u32[]{:S(2)}, u32[]{:S(2)}) collective-permute-start(bf16[256,1024]{0,1:T(8,128)(2,1)S(1)} %collective-permute-done.2), channel_id=1, source_target_pairs={{0,1},{1,2},{2,3},{3,4},{4,5},{5,6},{6,7},{7,0},{8,9},{9,10},{10,1... | collective-permute-start | bytes 1572872 | tf_op jit(solution)/shard_map/ppermute | solution.py:18
  50.9 19.1 %copy-start.4 = (bf16[256,1024]{0,1:T(8,128)(2,1)}, bf16[256,1024]{0,1:T(8,128)(2,1)S(1)}, u32[]{:S(2)}) copy-start(bf16[256,1024]{0,1:T(8,128)(2,1)S(1)} %collective-permute-done.3) | copy-start | bytes 1572868
  50.9 9.5 %collective-permute-start.4 = (bf16[256,1024]{0,1:T(8,128)(2,1)S(1)}, bf16[256,1024]{0,1:T(8,128)(2,1)S(1)}, u32[]{:S(2)}, u32[]{:S(2)}) collective-permute-start(bf16[256,1024]{0,1:T(8,128)(2,1)S(1)} %collective-permute-done.3), channel_id=1, source_target_pairs={{0,1},{1,2},{2,3},{3,4},{4,5},{5,6},{6,7},{7,0},{8,9},{9,10},{10,1... | collective-permute-start | bytes 1572872 | tf_op jit(solution)/shard_map/ppermute | solution.py:18
  60.4 9.6 %copy-start.6 = (bf16[256,1024]{0,1:T(8,128)(2,1)}, bf16[256,1024]{0,1:T(8,128)(2,1)S(1)}, u32[]{:S(2)}) copy-start(bf16[256,1024]{0,1:T(8,128)(2,1)S(1)} %collective-permute-done.4) | copy-start | bytes 1572868
  60.4 9.6 %collective-permute-start.5 = (bf16[256,1024]{0,1:T(8,128)(2,1)S(1)}, bf16[256,1024]{0,1:T(8,128)(2,1)}, u32[]{:S(2)}, u32[]{:S(2)}) collective-permute-start(bf16[256,1024]{0,1:T(8,128)(2,1)S(1)} %collective-permute-done.4), channel_id=1, source_target_pairs={{0,1},{1,2},{2,3},{3,4},{4,5},{5,6},{6,7},{7,0},{8,9},{9,10},{10,1... | collective-permute-start | bytes 1572872 | tf_op jit(solution)/shard_map/ppermute | solution.py:18
  70.0 20.0 %collective-permute-start.6 = (bf16[256,1024]{0,1:T(8,128)(2,1)}, bf16[256,1024]{0,1:T(8,128)(2,1)}, u32[]{:S(2)}, u32[]{:S(2)}) collective-permute-start(bf16[256,1024]{0,1:T(8,128)(2,1)} %collective-permute-done.5), channel_id=1, source_target_pairs={{0,1},{1,2},{2,3},{3,4},{4,5},{5,6},{6,7},{7,0},{8,9},{9,10},{10,1... | collective-permute-start | bytes 1572872 | tf_op jit(solution)/shard_map/ppermute | solution.py:18
  86.3 10.5 %copy-start.7 = (bf16[256,1024]{0,1:T(8,128)(2,1)S(1)}, bf16[256,1024]{0,1:T(8,128)(2,1)}, u32[]{:S(2)}) copy-start(bf16[256,1024]{0,1:T(8,128)(2,1)} %copy-done.6) | copy-start | bytes 1572868
  86.3 10.6 %copy-start.5 = (bf16[256,1024]{0,1:T(8,128)(2,1)S(1)}, bf16[256,1024]{0,1:T(8,128)(2,1)}, u32[]{:S(2)}) copy-start(bf16[256,1024]{0,1:T(8,128)(2,1)} %copy-done.4) | copy-start | bytes 1572868
  116.6 285.5 %copy-start.1 = (s32[2,4]{1,0:T(2,128)S(1)}, s32[2,4]{1,0:T(2,128)}, u32[]{:S(2)}) copy-start(s32[2,4]{1,0:T(2,128)} %param.7) | copy-start | bytes 100
Sparse Core Ops, SparseCore 0:
  9.9 27.1 all-gather.4
  39.3 46.9 all-gather.2
  111.3 278.5 reduce-scatter.1
